TPU v7x, 32 devices: a whole 2x2x4 slice. The times are simulated.
32 devices in a mesh: pb: 2 (over x), ka: 16 (over z, y, core).
Axes of the slice: x: 2, y: 2, z: 4, core: 2. Of those that a mesh axis runs over, the one named last changes fastest.
Arguments:
- coupling: bfloat16 [5120, 2, 2048], P('ka', 'pb'), may hold values from -0.009765625 to 0.009765625
- eigvec: float32 [16, 2048], P('ka'), may hold values from -0.75 to 0.75
- energies: float32 [16, 32], P('ka'), may hold values from -1 to 1
- k_coords: int32 [3, 16], replicated, may hold values from 0 to 63
- r_coords: int32 [3, 5120], P(None, 'ka'), may hold values from -12 to 12
- degeneracy: int32 [5120], P('ka'), may hold values from 1 to 8
- kq_index: int32 [16, 24], P('ka', 'pb'), may hold values from 0 to 15
- omega: float32 [24, 2], P('pb'), may hold values from 0.05 to 0.5
- phonon_modes: float32 [24, 2, 2], P('pb'), may hold values from -4 to 4
Outputs:
- sigma: float32 [16, 32], P('ka', 'pb')
All inputs are finite; a program needn't handle non-finite values.
Results may differ from a plain program's by a relative error of at most 0.0013.
Values may be sent and summed in bfloat16 or wider, within the bound.
No kernel may reach another device: no remote copies, remote signals or barrier semaphores. Data moves between devices by JAX's collectives and lax.ppermute only.
A program may use at most 64 MiB of HBM per device.

v0:
```python
import math
import jax
import jax.numpy as jnp
from jax import lax
from jax.sharding import PartitionSpec as P

KGRID = 64
THERMAL = 0.1
SMEARING = 0.05
HIGHEST = lax.Precision.HIGHEST


def phases(k_coords, r_coords, degeneracy):
    turns = (
        k_coords[0][:, None] * r_coords[0][None, :]
        + k_coords[1][:, None] * r_coords[1][None, :]
        + k_coords[2][:, None] * r_coords[2][None, :]
    ) % KGRID
    angle = turns.astype(jnp.float32) * (2.0 * math.pi / KGRID)
    inverse = 1.0 / degeneracy.astype(jnp.float32)
    cosine = (jnp.cos(angle) * inverse[None, :]).astype(jnp.bfloat16)
    sine = (jnp.sin(angle) * inverse[None, :]).astype(jnp.bfloat16)
    return (cosine, sine)


def combine_parts(cosine_sum, sine_sum, modes, square):
    cosine_rows = cosine_sum.reshape(cosine_sum.shape[0], modes, 2, square)
    sine_rows = sine_sum.reshape(sine_sum.shape[0], modes, 2, square)
    real_part = cosine_rows[:, :, 0] - sine_rows[:, :, 1]
    imag_part = cosine_rows[:, :, 1] + sine_rows[:, :, 0]
    return jnp.stack([real_part, imag_part], axis=2).reshape(
        cosine_sum.shape[0], modes * 2 * square
    )


def lorentz(spacing):
    return SMEARING / (math.pi * (spacing * spacing + SMEARING * SMEARING))


def self_energy(wannier, vector, energy, kq_vectors, kq_energies, omega, phonon):
    bands = energy.shape[0]
    modes = wannier.shape[0]
    matrix = wannier.astype(jnp.float32).reshape(modes, 2, bands, bands)
    rotate = vector.reshape(2, bands, bands)
    fold_real = jnp.einsum("vac,cn->van", matrix[:, 0], rotate[0], precision=HIGHEST) - jnp.einsum(
        "vac,cn->van", matrix[:, 1], rotate[1], precision=HIGHEST
    )
    fold_imag = jnp.einsum("vac,cn->van", matrix[:, 0], rotate[1], precision=HIGHEST) + jnp.einsum(
        "vac,cn->van", matrix[:, 1], rotate[0], precision=HIGHEST
    )
    mixed_real = jnp.einsum("qwv,wan->qvan", phonon, fold_real, precision=HIGHEST)
    mixed_imag = jnp.einsum("qwv,wan->qvan", phonon, fold_imag, precision=HIGHEST)
    target = kq_vectors.reshape(-1, 2, bands, bands)
    final_real = jnp.einsum(
        "qam,qvan->qmvn", target[:, 0], mixed_real, precision=HIGHEST
    ) + jnp.einsum("qam,qvan->qmvn", target[:, 1], mixed_imag, precision=HIGHEST)
    final_imag = jnp.einsum(
        "qam,qvan->qmvn", target[:, 0], mixed_imag, precision=HIGHEST
    ) - jnp.einsum("qam,qvan->qmvn", target[:, 1], mixed_real, precision=HIGHEST)
    strength = final_real * final_real + final_imag * final_imag
    fermi = 1.0 / (1.0 + jnp.exp(kq_energies / THERMAL))
    bose = 1.0 / jnp.expm1(omega / THERMAL)
    spacing = energy[None, None, None, :] - kq_energies[:, :, None, None]
    absorb = lorentz(spacing + omega[:, None, :, None])
    emit = lorentz(spacing - omega[:, None, :, None])
    bose_wide = bose[:, None, :, None]
    fermi_wide = fermi[:, :, None, None]
    occupy = (bose_wide + fermi_wide) * absorb + (bose_wide + 1.0 - fermi_wide) * emit
    return jnp.sum(strength * occupy, axis=(0, 1, 2))


def fourier_terms(k_coords, r_coords, degeneracy, slab, modes, square, count):
    cosine, sine = phases(k_coords, r_coords, degeneracy)
    stacked = jnp.dot(
        jnp.concatenate([cosine, sine], axis=0), slab, preferred_element_type=jnp.float32
    )
    return combine_parts(stacked[:count], stacked[count:], modes, square)


def shards(
    coupling, eigvec, energies, k_coords, r_coords, degeneracy, kq_index, omega, phonon_modes
):
    bands = energies.shape[1]
    points = eigvec.shape[0]
    local_modes = coupling.shape[1]
    slab = coupling.reshape(coupling.shape[0], -1)
    partial_value = lax.psum_scatter(
        fourier_terms(
            k_coords,
            r_coords,
            degeneracy,
            slab,
            local_modes,
            bands * bands,
            points * lax.axis_size("ka"),
        ),
        "ka",
        scatter_dimension=0,
        tiled=True,
    )
    own_wannier = partial_value.astype(jnp.bfloat16).reshape(points, local_modes, 2 * bands * bands)
    wannier = lax.all_gather(own_wannier, "pb", axis=1, tiled=True)
    pairs = kq_index.reshape(-1)
    pieces = (
        lax.all_gather(eigvec, "ka", axis=0, tiled=True),
        lax.all_gather(energies, "ka", axis=0, tiled=True),
    )
    labels = jnp.arange(pieces[0].shape[0], dtype=jnp.int32)
    hits = (pairs[:, None] == labels[None, :]).astype(jnp.float32)
    vectors_sum = jnp.dot(hits, pieces[0], precision=HIGHEST, preferred_element_type=jnp.float32)
    energy_sum = jnp.dot(hits, pieces[1], precision=HIGHEST, preferred_element_type=jnp.float32)
    kq_vectors = vectors_sum
    kq_energies = energy_sum
    queries = kq_index.shape[1]
    kq_vectors = kq_vectors.reshape(points, queries, eigvec.shape[1])
    kq_energies = kq_energies.reshape(points, queries, bands)

    def per_point(items):
        wannier_row, vector, energy, kq_rows, kq_levels = items
        return self_energy(wannier_row, vector, energy, kq_rows, kq_levels, omega, phonon_modes)

    sigma = lax.map(per_point, (wannier, eigvec, energies, kq_vectors, kq_energies))
    sigma = sigma / (queries * lax.axis_size("pb"))
    return lax.psum_scatter(sigma, "pb", scatter_dimension=1, tiled=True)


def solution(mesh):
    in_specs = (
        P("ka", "pb", None),
        P("ka", None),
        P("ka", None),
        P(),
        P(None, "ka"),
        P("ka"),
        P("ka", "pb"),
        P("pb", None),
        P("pb", None, None),
    )
    out_specs = P("ka", "pb")
    return jax.shard_map(shards, mesh=mesh, in_specs=in_specs, out_specs=out_specs, check_vma=False)
```

profile of v0, /device:TPU:0, one launch (start us, length us, event | category | flops | bytes accessed | tf_op | source)
XLA Modules:
  0.0 140.0 jit_solution(4159584743243929971)
XLA Ops:
  6.5 0.8 broadcast_add_fusion.1
  7.3 0.8 copy.45
  8.1 0.8 slice_reduce_fusion.4
  8.9 0.8 slice_bitcast_fusion.14
  9.7 0.7 convert_divide_fusion
  10.4 0.2 multiply_convert_fusion.1
  10.6 0.3 fusion
  11.2 0.1 slice_subtract_fusion
  11.4 0.1 pad_maximum_fusion
  11.6 63.8 %all-reduce.2 = bf16[16,2048]{1,0:T(8,128)(2,1)S(1)} all-reduce(f32[16,2048]{1,0:T(8,128)S(1)} %bitcast.78), channel_id=3, replica_groups=mesh['pb'=2,'ka'=16] {'ka'}, use_global_device_ids=true, to_apply=%region_0.1.clone | all-reduce | flops 32768 | bytes 196608
  75.4 0.6 dynamic-slice.2
  76.0 0.7 fusion.28
  76.6 4.4 %all-gather.2 = bf16[2,1,2048]{2,1,0:T(2,128)(2,1)S(1)} all-gather(bf16[1,1,2048]{2,1,0:T(2,128)(2,1)S(1)} %fusion.28), channel_id=2, replica_groups=mesh['pb'=2,'ka'=16] {'pb'}, dimensions={0}, use_global_device_ids=true | all-gather | bytes 12288 | tf_op jit(solution)/shard_map/all_gather | solution.py:102
  81.3 0.1 fusion.27
  81.5 0.1 fusion.26
  81.6 0.1 fusion.8
  81.8 17.5 %all-gather.1 = f32[16,1,2048]{2,1,0:T(1,128)S(1)} all-gather(f32[1,1,2048]{2,1,0:T(1,128)S(1)} %bitcast.80), channel_id=1, replica_groups=mesh['pb'=2,'ka'=16] {'ka'}, dimensions={0}, use_global_device_ids=true | all-gather | bytes 139264 | tf_op jit(solution)/shard_map/all_gather | solution.py:105
  99.3 0.3 fusion.15
  99.5 0.1 reshape.87
  99.7 0.1 fusion.7
  99.8 0.6 convolution_bitcast_fusion.1
  100.4 0.6 convolution_bitcast_fusion
  101.1 0.7 fusion.13
  101.8 0.7 fusion.9
  102.5 0.7 fusion.2
  103.2 19.1 %all-gather.3 = f32[16,1,32]{2,1,0:T(1,128)S(1)} all-gather(f32[1,1,32]{2,1,0:T(1,128)S(1)} %bitcast.83), channel_id=1, replica_groups=mesh['pb'=2,'ka'=16] {'ka'}, dimensions={0}, use_global_device_ids=true | all-gather | bytes 2176 | tf_op jit(solution)/shard_map/all_gather | solution.py:106
  122.2 0.2 add_divide_fusion
  122.6 0.1 broadcast_subtract_fusion
  122.9 1.0 fusion.6
  123.8 0.7 copy.55
  124.5 7.3 %reduce-scatter.4.cloned.1.call-done = f32[16,1]{1,0:T(8,128)} async-done(((f32[32,1]{1,0:T(8,128)}), f32[16,1]{1,0:T(8,128)}) %reduce-scatter.4.cloned.1.call-update) | async-done | bytes 80
  131.9 1.3 copy.56
  (27 shorter events, 0.9 us)
Async XLA Ops:
  6.5 4.1 %copy-start = (bf16[320,1,2048]{2,0,1:T(8,128)(2,1)S(1)}, bf16[320,1,2048]{2,0,1:T(8,128)(2,1)}, u32[]{:S(2)}) copy-start(bf16[320,1,2048]{2,0,1:T(8,128)(2,1)} %param.9) | copy-start | bytes 3932164
  6.5 125.3 %reduce-scatter.4.cloned.1.call-start = ((), (), s32[]{:S(2)}) async-start(), calls=%async_computation.1 | async-start | bytes 24576
  10.9 64.4 %copy-start.5 = (u32[32]{0:T(128)S(1)}, u32[32]{0:T(128)}, u32[]{:S(2)}) copy-start(u32[32]{0:T(128)} %constant.68) | copy-start | bytes 388
  10.9 70.2 %copy-start.1 = (f32[1,2048]{1,0:T(1,128)S(1)}, f32[1,2048]{1,0:T(1,128)}, u32[]{:S(2)}) copy-start(f32[1,2048]{1,0:T(1,128)} %param.10) | copy-start | bytes 24580
  11.0 88.3 %copy-start.4 = (s32[1,12]{1,0:T(1,128)S(1)}, s32[1,12]{1,0:T(1,128)}, u32[]{:S(2)}) copy-start(s32[1,12]{1,0:T(1,128)} %param.15) | copy-start | bytes 148
  11.2 88.6 %copy-start.2 = (f32[12,2,2]{0,2,1:T(2,128)S(1)}, f32[12,2,2]{0,2,1:T(2,128)}, u32[]{:S(2)}) copy-start(f32[12,2,2]{0,2,1:T(2,128)} %param.17) | copy-start | bytes 580
  101.8 1.4 copy-start.3
Sparse Core Ops, SparseCore 0:
  124.7 7.1 reduce-scatter.3
where the time goes:
time: 140 us
  blocking collectives  105 us (75%)
  between operations  13.6 us (10%)
  waiting for transfers between devices  7.35 us (5%)
  local copies, waits for them, and re-layouts  6.51 us (5%)
  matrix products  5.57 us (4%)
  other arithmetic  2.19 us (2%)
    unnamed x1, blocking collectives  63.8 us
    all_gather x1, blocking collectives, shards(): lax.all_gather(energies, 'ka', axis=0, tiled=True)  19.1 us
    all_gather x1, blocking collectives, shards(): lax.all_gather(eigvec, 'ka', axis=0, tiled=True)  17.5 us
    unnamed x2, waiting for transfers between devices  7.35 us
    all_gather x1, blocking collectives, shards(): wannier = lax.all_gather(own_wannier, 'pb', axis=1, tiled=True)  4.36 us
    unnamed x18, local copies, waits for them, and re-layouts  4.06 us
  transfers between devices with their start and end apart: 1, of which 1 were waited for; matrix products, arithmetic and copies ran while one was open for 0% of the time, Pallas kernels for 0%

commit v1 on v0

--- a/solution.py
+++ b/solution.py
@@ -101,10 +101,34 @@
     own_wannier = partial_value.astype(jnp.bfloat16).reshape(points, local_modes, 2 * bands * bands)
     wannier = lax.all_gather(own_wannier, "pb", axis=1, tiled=True)
     pairs = kq_index.reshape(-1)
-    pieces = (
-        lax.all_gather(eigvec, "ka", axis=0, tiled=True),
-        lax.all_gather(energies, "ka", axis=0, tiled=True),
-    )
+
+    def refer_the_panels(view, axis_no):
+        upper = lax.psum(1, axis_name="ka")
+        state_now = lax.axis_index("ka")
+        piece_now, part_now, outer = (upper, state_now, view.shape[axis_no])
+        by_rank = [ix * piece_now if c == axis_no else ix for c, ix in enumerate(view.shape)]
+        w2 = jnp.zeros(by_rank, view.dtype)
+        high = lax.dynamic_update_slice_in_dim(w2, view, part_now * outer, axis=axis_no)
+        last = carry_in = view
+        for no in range(1, piece_now // 2 + 1):
+            last = lax.ppermute(
+                last, axis_name="ka", perm=[(c, (c + 1) % piece_now) for c in range(piece_now)]
+            )
+            high = lax.dynamic_update_slice_in_dim(
+                high, last, (part_now - no) % piece_now * outer, axis=axis_no
+            )
+            if 2 * no < piece_now:
+                carry_in = lax.ppermute(
+                    carry_in,
+                    axis_name="ka",
+                    perm=[(c, (c - 1) % piece_now) for c in range(piece_now)],
+                )
+                high = lax.dynamic_update_slice_in_dim(
+                    high, carry_in, (part_now + no) % piece_now * outer, axis=axis_no
+                )
+        return high
+
+    pieces = (lax.all_gather(eigvec, "ka", axis=0, tiled=True), refer_the_panels(energies, 0))
     labels = jnp.arange(pieces[0].shape[0], dtype=jnp.int32)
     hits = (pairs[:, None] == labels[None, :]).astype(jnp.float32)
     vectors_sum = jnp.dot(hits, pieces[0], precision=HIGHEST, preferred_element_type=jnp.float32)

time: 140 us -> 163 us (1.16)
  starting transfers between devices: 0.01 us -> 32 us
  blocking collectives: 105 us -> 80.8 us
  waiting for transfers between devices: 7.35 us -> 20.4 us
    ppermute x0 -> x15, starting transfers between devices: none -> 32 us  [the longest x7 31.1 us: refer_the_panels(): lax.ppermute(carry_in, axis_name='ka', perm=[(c, (c - 1) % piece_now) for...]
    all_gather x1 -> x0, blocking collectives: 19.1 us -> none  [shards(): lax.all_gather(energies, 'ka', axis=0, tiled=True)]
    ppermute x0 -> x15, waiting for transfers between devices: none -> 13 us  [the longest x8 12.8 us: refer_the_panels(): lax.ppermute(last, axis_name='ka', perm=[(c, (c + 1) % piece_now) for c i...]
    unnamed x1, blocking collectives: 63.8 us -> 59 us
  transfers between devices with their start and end apart: 1 -> 16, of which waited for: 1 -> 8; matrix products, arithmetic and copies ran while one was open for 0% -> 7% of each run, Pallas kernels for 0% -> 0%
where the time goes in v1:
time: 163 us; the launch traced here: 162 us
  blocking collectives  80.8 us (50%)
  starting transfers between devices  32 us (20%)
  waiting for transfers between devices  20.4 us (13%)
  between operations  13.7 us (8%)
  local copies, waits for them, and re-layouts  7.64 us (5%)
  matrix products  5.56 us (3%)
  other arithmetic  2.09 us (1%)
    unnamed x1, blocking collectives  59 us
    ppermute x7, starting transfers between devices, refer_the_panels(): lax.ppermute(carry_in, axis_name='ka', perm=[(c, (c - 1) % piece_now) for...  31.1 us
    all_gather x1, blocking collectives, shards(): lax.all_gather(eigvec, 'ka', axis=0, tiled=True)  17.5 us
    ppermute x8, waiting for transfers between devices, refer_the_panels(): lax.ppermute(last, axis_name='ka', perm=[(c, (c + 1) % piece_now) for c i...  12.8 us
    unnamed x2, waiting for transfers between devices  7.37 us
    all_gather x1, blocking collectives, shards(): wannier = lax.all_gather(own_wannier, 'pb', axis=1, tiled=True)  4.36 us
    unnamed x18, local copies, waits for them, and re-layouts  4.07 us
  transfers between devices with their start and end apart: 16, of which 8 were waited for; matrix products, arithmetic and copies ran while one was open for 7% of the time, Pallas kernels for 0%

profile of v1, /device:TPU:0, one launch (start us, length us, event | category | flops | bytes accessed | tf_op | source)
XLA Modules:
  0.0 162.2 jit_solution(8904176005077034815)
XLA Ops:
  7.0 5.0 %collective-permute-start.1 = (f32[1,32]{1,0:T(1,128)}, f32[1,32]{1,0:T(1,128)S(1)}, u32[]{:S(2)}, u32[]{:S(2)}) collective-permute-start(f32[1,32]{1,0:T(1,128)} %param.11), channel_id=1, source_target_pairs={{0,15},{1,0},{2,1},{3,2},{4,3},{5,4},{6,5},{7,6},{8,7},{9,8},{10,9... | collective-permute-start | bytes 392 | tf_op jit(solution)/shard_map/ppermute | solution.py:121
  12.0 0.7 broadcast_add_fusion.1
  12.7 0.8 copy.45
  13.5 0.7 slice_reduce_fusion.1
  14.3 0.7 convert_divide_fusion
  15.0 0.8 slice_reduce_fusion.4
  15.8 0.8 slice_bitcast_fusion.14
  17.7 59.0 %all-reduce.2 = bf16[16,2048]{1,0:T(8,128)(2,1)S(1)} all-reduce(f32[16,2048]{1,0:T(8,128)S(1)} %bitcast.76), channel_id=3, replica_groups=mesh['pb'=2,'ka'=16] {'ka'}, use_global_device_ids=true, to_apply=%region_0.1.clone | all-reduce | flops 32768 | bytes 196608
  77.3 0.7 fusion.28
  78.0 4.4 %all-gather.2 = bf16[2,1,2048]{2,1,0:T(2,128)(2,1)S(1)} all-gather(bf16[1,1,2048]{2,1,0:T(2,128)(2,1)S(1)} %fusion.28), channel_id=2, replica_groups=mesh['pb'=2,'ka'=16] {'pb'}, dimensions={0}, use_global_device_ids=true | all-gather | bytes 12288 | tf_op jit(solution)/shard_map/all_gather | solution.py:102
  83.0 17.5 %all-gather.1 = f32[16,1,2048]{2,1,0:T(1,128)S(1)} all-gather(f32[1,1,2048]{2,1,0:T(1,128)S(1)} %bitcast.78), channel_id=1, replica_groups=mesh['pb'=2,'ka'=16] {'ka'}, dimensions={0}, use_global_device_ids=true | all-gather | bytes 139264 | tf_op jit(solution)/shard_map/all_gather | solution.py:131
  101.1 0.6 convolution_bitcast_fusion
  102.3 0.7 fusion.9
  103.0 0.7 fusion.13
  103.7 0.7 fusion.2
  105.1 4.1 %collective-permute-start.3 = (f32[1,32]{1,0:T(1,128)S(1)}, f32[1,32]{1,0:T(1,128)S(1)}, u32[]{:S(2)}, u32[]{:S(2)}) collective-permute-start(f32[1,32]{1,0:T(1,128)S(1)} %collective-permute-done.1), channel_id=1, source_target_pairs={{0,15},{1,0},{2,1},{3,2},{4,3},{5,4},{6,5},{7,6},{8,7},{9,8},{10,9... | collective-permute-start | bytes 392 | tf_op jit(solution)/shard_map/ppermute | solution.py:121
  109.3 1.2 collective-permute-done.2
  110.5 4.4 %collective-permute-start.5 = (f32[1,32]{1,0:T(1,128)S(1)}, f32[1,32]{1,0:T(1,128)S(1)}, u32[]{:S(2)}, u32[]{:S(2)}) collective-permute-start(f32[1,32]{1,0:T(1,128)S(1)} %collective-permute-done.3), channel_id=1, source_target_pairs={{0,15},{1,0},{2,1},{3,2},{4,3},{5,4},{6,5},{7,6},{8,7},{9,8},{10,9... | collective-permute-start | bytes 392 | tf_op jit(solution)/shard_map/ppermute | solution.py:121
  115.0 1.2 collective-permute-done.4
  116.2 4.4 %collective-permute-start.7 = (f32[1,32]{1,0:T(1,128)S(1)}, f32[1,32]{1,0:T(1,128)S(1)}, u32[]{:S(2)}, u32[]{:S(2)}) collective-permute-start(f32[1,32]{1,0:T(1,128)S(1)} %collective-permute-done.5), channel_id=1, source_target_pairs={{0,15},{1,0},{2,1},{3,2},{4,3},{5,4},{6,5},{7,6},{8,7},{9,8},{10,9... | collective-permute-start | bytes 392 | tf_op jit(solution)/shard_map/ppermute | solution.py:121
  120.7 1.2 collective-permute-done.6
  121.9 4.4 %collective-permute-start.9 = (f32[1,32]{1,0:T(1,128)S(1)}, f32[1,32]{1,0:T(1,128)S(1)}, u32[]{:S(2)}, u32[]{:S(2)}) collective-permute-start(f32[1,32]{1,0:T(1,128)S(1)} %collective-permute-done.7), channel_id=1, source_target_pairs={{0,15},{1,0},{2,1},{3,2},{4,3},{5,4},{6,5},{7,6},{8,7},{9,8},{10,9... | collective-permute-start | bytes 392 | tf_op jit(solution)/shard_map/ppermute | solution.py:121
  126.4 1.2 collective-permute-done.8
  127.6 4.4 %collective-permute-start.11 = (f32[1,32]{1,0:T(1,128)S(1)}, f32[1,32]{1,0:T(1,128)S(1)}, u32[]{:S(2)}, u32[]{:S(2)}) collective-permute-start(f32[1,32]{1,0:T(1,128)S(1)} %collective-permute-done.9), channel_id=1, source_target_pairs={{0,15},{1,0},{2,1},{3,2},{4,3},{5,4},{6,5},{7,6},{8,7},{9,8},{10,9... | collective-permute-start | bytes 392 | tf_op jit(solution)/shard_map/ppermute | solution.py:121
  132.1 1.2 collective-permute-done.10
  133.3 4.4 %collective-permute-start.13 = (f32[1,32]{1,0:T(1,128)S(1)}, f32[1,32]{1,0:T(1,128)S(1)}, u32[]{:S(2)}, u32[]{:S(2)}) collective-permute-start(f32[1,32]{1,0:T(1,128)S(1)} %collective-permute-done.11), channel_id=1, source_target_pairs={{0,15},{1,0},{2,1},{3,2},{4,3},{5,4},{6,5},{7,6},{8,7},{9,8},{10,9... | collective-permute-start | bytes 392 | tf_op jit(solution)/shard_map/ppermute | solution.py:121
  137.7 1.2 collective-permute-done.12
  139.0 5.6 %collective-permute-done.14 = f32[1,32]{1,0:T(1,128)S(1)} collective-permute-done((f32[1,32]{1,0:T(1,128)S(1)}, f32[1,32]{1,0:T(1,128)S(1)}, u32[]{:S(2)}, u32[]{:S(2)}) %collective-permute-start.14) | collective-permute-done | bytes 160 | tf_op jit(solution)/shard_map/ppermute | solution.py:114
  145.1 0.9 fusion.6
  146.0 0.7 copy.55
  146.8 7.4 %reduce-scatter.4.cloned.1.call-done = f32[16,1]{1,0:T(8,128)} async-done(((f32[32,1]{1,0:T(8,128)}), f32[16,1]{1,0:T(8,128)}) %reduce-scatter.4.cloned.1.call-update) | async-done | bytes 80
  154.1 1.3 copy.56
  (73 shorter events, 5.7 us)
Async XLA Ops:
  6.5 10.3 %copy-start = (bf16[320,1,2048]{2,0,1:T(8,128)(2,1)S(1)}, bf16[320,1,2048]{2,0,1:T(8,128)(2,1)}, u32[]{:S(2)}) copy-start(bf16[320,1,2048]{2,0,1:T(8,128)(2,1)} %param.9) | copy-start | bytes 3932164
  6.5 147.6 %reduce-scatter.4.cloned.1.call-start = ((), (), s32[]{:S(2)}) async-start(), calls=%async_computation.1 | async-start | bytes 24576
  6.5 98.2 %collective-permute-start = (f32[1,32]{1,0:T(1,128)}, f32[1,32]{1,0:T(1,128)S(1)}, u32[]{:S(2)}, u32[]{:S(2)}) collective-permute-start(f32[1,32]{1,0:T(1,128)} %param.11), channel_id=1, source_target_pairs={{0,1},{1,2},{2,3},{3,4},{4,5},{5,6},{6,7},{7,8},{8,9},{9,10},{10,1... | collective-permute-start | bytes 392 | tf_op jit(solution)/shard_map/ppermute | solution.py:114
  7.0 98.1 %collective-permute-start.1 = (f32[1,32]{1,0:T(1,128)}, f32[1,32]{1,0:T(1,128)S(1)}, u32[]{:S(2)}, u32[]{:S(2)}) collective-permute-start(f32[1,32]{1,0:T(1,128)} %param.11), channel_id=1, source_target_pairs={{0,15},{1,0},{2,1},{3,2},{4,3},{5,4},{6,5},{7,6},{8,7},{9,8},{10,9... | collective-permute-start | bytes 392 | tf_op jit(solution)/shard_map/ppermute | solution.py:121
  17.1 59.6 %copy-start.5 = (u32[32]{0:T(128)S(1)}, u32[32]{0:T(128)}, u32[]{:S(2)}) copy-start(u32[32]{0:T(128)} %constant.172) | copy-start | bytes 388
  17.1 65.9 %copy-start.1 = (f32[1,2048]{1,0:T(1,128)S(1)}, f32[1,2048]{1,0:T(1,128)}, u32[]{:S(2)}) copy-start(f32[1,2048]{1,0:T(1,128)} %param.10) | copy-start | bytes 24580
  17.1 83.4 %copy-start.4 = (s32[1,12]{1,0:T(1,128)S(1)}, s32[1,12]{1,0:T(1,128)}, u32[]{:S(2)}) copy-start(s32[1,12]{1,0:T(1,128)} %param.15) | copy-start | bytes 148
  17.4 83.7 %copy-start.2 = (f32[12,2,2]{0,2,1:T(2,128)S(1)}, f32[12,2,2]{0,2,1:T(2,128)}, u32[]{:S(2)}) copy-start(f32[12,2,2]{0,2,1:T(2,128)} %param.17) | copy-start | bytes 580
  103.0 1.6 copy-start.3
  104.7 5.7 %collective-permute-start.2 = (f32[1,32]{1,0:T(1,128)S(1)}, f32[1,32]{1,0:T(1,128)S(1)}, u32[]{:S(2)}, u32[]{:S(2)}) collective-permute-start(f32[1,32]{1,0:T(1,128)S(1)} %collective-permute-done), channel_id=1, source_target_pairs={{0,1},{1,2},{2,3},{3,4},{4,5},{5,6},{6,7},{7,8},{8,9},{9,10},{10,1... | collective-permute-start | bytes 392 | tf_op jit(solution)/shard_map/ppermute | solution.py:114
  105.1 5.4 %collective-permute-start.3 = (f32[1,32]{1,0:T(1,128)S(1)}, f32[1,32]{1,0:T(1,128)S(1)}, u32[]{:S(2)}, u32[]{:S(2)}) collective-permute-start(f32[1,32]{1,0:T(1,128)S(1)} %collective-permute-done.1), channel_id=1, source_target_pairs={{0,15},{1,0},{2,1},{3,2},{4,3},{5,4},{6,5},{7,6},{8,7},{9,8},{10,9... | collective-permute-start | bytes 392 | tf_op jit(solution)/shard_map/ppermute | solution.py:121
  110.5 5.7 %collective-permute-start.4 = (f32[1,32]{1,0:T(1,128)S(1)}, f32[1,32]{1,0:T(1,128)S(1)}, u32[]{:S(2)}, u32[]{:S(2)}) collective-permute-start(f32[1,32]{1,0:T(1,128)S(1)} %collective-permute-done.2), channel_id=1, source_target_pairs={{0,1},{1,2},{2,3},{3,4},{4,5},{5,6},{6,7},{7,8},{8,9},{9,10},{10,1... | collective-permute-start | bytes 392 | tf_op jit(solution)/shard_map/ppermute | solution.py:114
  110.5 5.7 %collective-permute-start.5 = (f32[1,32]{1,0:T(1,128)S(1)}, f32[1,32]{1,0:T(1,128)S(1)}, u32[]{:S(2)}, u32[]{:S(2)}) collective-permute-start(f32[1,32]{1,0:T(1,128)S(1)} %collective-permute-done.3), channel_id=1, source_target_pairs={{0,15},{1,0},{2,1},{3,2},{4,3},{5,4},{6,5},{7,6},{8,7},{9,8},{10,9... | collective-permute-start | bytes 392 | tf_op jit(solution)/shard_map/ppermute | solution.py:121
  116.2 5.7 %collective-permute-start.6 = (f32[1,32]{1,0:T(1,128)S(1)}, f32[1,32]{1,0:T(1,128)S(1)}, u32[]{:S(2)}, u32[]{:S(2)}) collective-permute-start(f32[1,32]{1,0:T(1,128)S(1)} %collective-permute-done.4), channel_id=1, source_target_pairs={{0,1},{1,2},{2,3},{3,4},{4,5},{5,6},{6,7},{7,8},{8,9},{9,10},{10,1... | collective-permute-start | bytes 392 | tf_op jit(solution)/shard_map/ppermute | solution.py:114
  116.2 5.7 %collective-permute-start.7 = (f32[1,32]{1,0:T(1,128)S(1)}, f32[1,32]{1,0:T(1,128)S(1)}, u32[]{:S(2)}, u32[]{:S(2)}) collective-permute-start(f32[1,32]{1,0:T(1,128)S(1)} %collective-permute-done.5), channel_id=1, source_target_pairs={{0,15},{1,0},{2,1},{3,2},{4,3},{5,4},{6,5},{7,6},{8,7},{9,8},{10,9... | collective-permute-start | bytes 392 | tf_op jit(solution)/shard_map/ppermute | solution.py:121
  121.9 5.7 %collective-permute-start.8 = (f32[1,32]{1,0:T(1,128)S(1)}, f32[1,32]{1,0:T(1,128)S(1)}, u32[]{:S(2)}, u32[]{:S(2)}) collective-permute-start(f32[1,32]{1,0:T(1,128)S(1)} %collective-permute-done.6), channel_id=1, source_target_pairs={{0,1},{1,2},{2,3},{3,4},{4,5},{5,6},{6,7},{7,8},{8,9},{9,10},{10,1... | collective-permute-start | bytes 392 | tf_op jit(solution)/shard_map/ppermute | solution.py:114
  121.9 5.7 %collective-permute-start.9 = (f32[1,32]{1,0:T(1,128)S(1)}, f32[1,32]{1,0:T(1,128)S(1)}, u32[]{:S(2)}, u32[]{:S(2)}) collective-permute-start(f32[1,32]{1,0:T(1,128)S(1)} %collective-permute-done.7), channel_id=1, source_target_pairs={{0,15},{1,0},{2,1},{3,2},{4,3},{5,4},{6,5},{7,6},{8,7},{9,8},{10,9... | collective-permute-start | bytes 392 | tf_op jit(solution)/shard_map/ppermute | solution.py:121
  127.6 5.7 %collective-permute-start.10 = (f32[1,32]{1,0:T(1,128)S(1)}, f32[1,32]{1,0:T(1,128)S(1)}, u32[]{:S(2)}, u32[]{:S(2)}) collective-permute-start(f32[1,32]{1,0:T(1,128)S(1)} %collective-permute-done.8), channel_id=1, source_target_pairs={{0,1},{1,2},{2,3},{3,4},{4,5},{5,6},{6,7},{7,8},{8,9},{9,10},{10,1... | collective-permute-start | bytes 392 | tf_op jit(solution)/shard_map/ppermute | solution.py:114
  127.6 5.7 %collective-permute-start.11 = (f32[1,32]{1,0:T(1,128)S(1)}, f32[1,32]{1,0:T(1,128)S(1)}, u32[]{:S(2)}, u32[]{:S(2)}) collective-permute-start(f32[1,32]{1,0:T(1,128)S(1)} %collective-permute-done.9), channel_id=1, source_target_pairs={{0,15},{1,0},{2,1},{3,2},{4,3},{5,4},{6,5},{7,6},{8,7},{9,8},{10,9... | collective-permute-start | bytes 392 | tf_op jit(solution)/shard_map/ppermute | solution.py:121
  133.2 5.7 %collective-permute-start.12 = (f32[1,32]{1,0:T(1,128)S(1)}, f32[1,32]{1,0:T(1,128)S(1)}, u32[]{:S(2)}, u32[]{:S(2)}) collective-permute-start(f32[1,32]{1,0:T(1,128)S(1)} %collective-permute-done.10), channel_id=1, source_target_pairs={{0,1},{1,2},{2,3},{3,4},{4,5},{5,6},{6,7},{7,8},{8,9},{9,10},{10,1... | collective-permute-start | bytes 392 | tf_op jit(solution)/shard_map/ppermute | solution.py:114
  133.3 5.7 %collective-permute-start.13 = (f32[1,32]{1,0:T(1,128)S(1)}, f32[1,32]{1,0:T(1,128)S(1)}, u32[]{:S(2)}, u32[]{:S(2)}) collective-permute-start(f32[1,32]{1,0:T(1,128)S(1)} %collective-permute-done.11), channel_id=1, source_target_pairs={{0,15},{1,0},{2,1},{3,2},{4,3},{5,4},{6,5},{7,6},{8,7},{9,8},{10,9... | collective-permute-start | bytes 392 | tf_op jit(solution)/shard_map/ppermute | solution.py:121
  138.9 5.7 %collective-permute-start.14 = (f32[1,32]{1,0:T(1,128)S(1)}, f32[1,32]{1,0:T(1,128)S(1)}, u32[]{:S(2)}, u32[]{:S(2)}) collective-permute-start(f32[1,32]{1,0:T(1,128)S(1)} %collective-permute-done.12), channel_id=1, source_target_pairs={{0,1},{1,2},{2,3},{3,4},{4,5},{5,6},{6,7},{7,8},{8,9},{9,10},{10,1... | collective-permute-start | bytes 392 | tf_op jit(solution)/shard_map/ppermute | solution.py:114
Sparse Core Ops, SparseCore 0:
  146.9 7.1 reduce-scatter.3
